TPU v7x, 128 devices: a whole 4x4x4 slice. The times are simulated.
128 devices in a mesh: wide: 16 (over x, y_hi, core), narrow: 8 (over z, y_lo).
Axes of the slice: x: 4, y: 4 (y_hi: 2, y_lo: 2; y = y_hi * 2 + y_lo), z: 4, core: 2. Of those that a mesh axis runs over, the one named last changes fastest.
Arguments:
- dosages: int32 [2048, 24576], P('narrow', 'wide'), may hold values from 0 to 3, as said below
- allele_counts: int32 [2048], P('narrow'), may hold values from 4000 to 384000, as said below
- called_counts: int32 [2048], P('narrow'), may hold values from 200000 to 400000
Outputs:
- relation: float32 [16, 8, 192, 24576], P(None, 'narrow', None, 'wide')
Inputs may be any that keep to these rules, and one draw needn't show every extreme that they name: 3 marks a missing call; 0, 1 and 2 are dosages. `allele_counts`: the floor of the SNP's called_counts times a whole number p from 1 to 48, divided by 50, so that freq lies in (0, 0.5).
All inputs are finite; a program needn't handle non-finite values.
Results may differ from a plain program's by a relative error of at most 0.0043.
Values may be sent and summed in bfloat16 or wider, within the bound.
A program may use at most 128 MiB of HBM per device.

v0:
```python
import jax
import jax.numpy as jnp
from jax import lax
from jax.sharding import PartitionSpec as P

SNPS = 2048


def standardize(dosages, allele_counts, called_counts):
    freq = allele_counts.astype(jnp.float32) / (2.0 * called_counts.astype(jnp.float32))
    freq = freq[:, None]
    values = (dosages.astype(jnp.float32) - 2.0 * freq) * lax.rsqrt(2.0 * freq * (1.0 - freq))
    values = jnp.where(dosages == 3, jnp.zeros_like(values), values)
    return values.astype(jnp.bfloat16)


def shards(dosages, allele_counts, called_counts):
    standard = standardize(dosages, allele_counts, called_counts)
    sub_width = standard.shape[1] // lax.axis_size("narrow")
    block_rows = lax.all_gather(standard, "narrow", axis=0, tiled=True)
    position = lax.axis_index("narrow") * sub_width
    panel = lax.dynamic_slice_in_dim(block_rows, position, sub_width, 1)
    col_count = block_rows.shape[1]
    gathered = lax.all_gather(panel, "wide", axis=1, tiled=True)
    result = (
        lax.dot_general(
            gathered, block_rows, (((0,), (0,)), ((), ())), preferred_element_type=jnp.float32
        )
        / SNPS
    )
    return result.reshape(lax.axis_size("wide"), 1, sub_width, col_count)


def solution(mesh):
    return jax.shard_map(
        shards,
        mesh=mesh,
        in_specs=(P("narrow", "wide"), P("narrow"), P("narrow")),
        out_specs=P(None, "narrow", None, "wide"),
        check_vma=False,
    )
```

profile of v0, /device:TPU:1, one launch (start us, length us, event | category | flops | bytes accessed | tf_op | source)
XLA Modules:
  0.0 269.7 jit_solution(2306122670743038809)
XLA Ops:
  6.5 0.0 all-gather.3.cloned.1.call-start
  6.5 0.7 broadcast_multiply_fusion
  7.2 1.9 copy.5
  9.1 1.2 select_convert_fusion
  10.3 0.0 all-gather.3.cloned.1.call-update
  10.3 0.0 all-gather.5.cloned.1.call-start
  10.4 131.8 %all-gather.3.cloned.1.call-done = bf16[2048,1536]{0,1:T(8,128)(2,1)} async-done(((bf16[256,1536]{0,1:T(8,128)(2,1)}), bf16[2048,1536]{0,1:T(8,128)(2,1)}) %all-gather.3.cloned.1.call-update) | async-done | bytes 6291472 | tf_op jit(solution)/shard_map/all_gather | solution.py:20
  142.2 2.1 constant_dynamic-slice_fusion
  144.3 0.0 all-gather.5.cloned.1.call-update
  144.4 92.3 %all-gather.5.cloned.1.call-done = bf16[2048,3072]{0,1:T(8,128)(2,1)} async-done(((bf16[2048,192]{0,1:T(8,128)(2,1)}), bf16[2048,3072]{0,1:T(8,128)(2,1)}) %all-gather.5.cloned.1.call-update) | async-done | bytes 12582928 | tf_op jit(solution)/shard_map/all_gather | solution.py:24
  236.6 26.2 %convolution_multiply_fusion = f32[3072,1536]{1,0:T(8,128)} fusion(bf16[2048,3072]{0,1:T(8,128)(2,1)} %all-gather.5.cloned.1.call-done, bf16[2048,1536]{0,1:T(8,128)(2,1)} %all-gather.3.cloned.1.call-done), kind=kOutput, calls=%fused_computation | convolution fusion | flops 19332071424 | bytes 37748736 | tf_op jit(solution)/shard_map/dot_general | solution.py:26
  (1 shorter events, 0.0 us)
Async XLA Ops:
  6.5 135.7 %all-gather.3.cloned.1.call-start = ((), (), s32[]{:S(2)}) async-start(), calls=%async_computation | async-start | bytes 7077888 | tf_op jit(solution)/shard_map/all_gather | solution.py:20
  10.3 226.3 %all-gather.5.cloned.1.call-start = ((), (), s32[]{:S(2)}) async-start(), calls=%async_computation.1 | async-start | bytes 13369344 | tf_op jit(solution)/shard_map/all_gather | solution.py:24
Sparse Core Ops, SparseCore 0:
  10.5 131.7 all-gather.2
  144.6 91.9 all-gather.4
where the time goes:
time: 270 us
  waiting for transfers between devices  224 us (83%)
  matrix products  26.2 us (10%)
  between operations  13.4 us (5%)
  local copies, waits for them, and re-layouts  3.97 us (1%)
    all_gather x1, waiting for transfers between devices, shards(): block_rows = lax.all_gather(standard, 'narrow', axis=0, tiled=True)  132 us
    all_gather x1, waiting for transfers between devices, shards(): gathered = lax.all_gather(panel, 'wide', axis=1, tiled=True)  92.3 us
    dot_general x1, matrix products, shards(): lax.dot_general(gathered, block_rows, (((0,), (0,)), ((), ())), preferred...  26.2 us
  transfers between devices with their start and end apart: 2, of which 2 were waited for; matrix products, arithmetic and copies ran while one was open for 0% of the time, Pallas kernels for 0%

commit v1 on v0

--- a/solution.py
+++ b/solution.py
@@ -21,7 +21,9 @@
     position = lax.axis_index("narrow") * sub_width
     panel = lax.dynamic_slice_in_dim(block_rows, position, sub_width, 1)
     col_count = block_rows.shape[1]
-    gathered = lax.all_gather(panel, "wide", axis=1, tiled=True)
+    gathered = jnp.concatenate(
+        lax.all_to_all(jnp.stack([panel] * lax.axis_size("wide")), "wide", 0, 0), axis=1
+    )
     result = (
         lax.dot_general(
             gathered, block_rows, (((0,), (0,)), ((), ())), preferred_element_type=jnp.float32

time: 270 us -> 332 us (1.23)
  blocking collectives: 0 us -> 148 us
  waiting for transfers between devices: 224 us -> 132 us
  local copies, waits for them, and re-layouts: 3.97 us -> 8.73 us
    all_to_all x0 -> x1, blocking collectives: none -> 148 us  [shards(): lax.all_to_all(jnp.stack([panel] * lax.axis_size('wide')), 'wide', 0, 0)]
    all_gather x1 -> x0, waiting for transfers between devices: 92.3 us -> none  [shards(): gathered = lax.all_gather(panel, 'wide', axis=1, tiled=True)]
    another operation x0 -> x1, local copies, waits for them, and re-layouts: none -> 6.38 us  [shards(): jnp.stack([panel] * lax.axis_size('wide'))]
  transfers between devices with their start and end apart: 2 -> 1, of which waited for: 2 -> 1; matrix products, arithmetic and copies ran while one was open for 0% -> 0% of each run, Pallas kernels for 0% -> 0%
where the time goes in v1:
time: 332 us; the launch traced here: 331 us
  blocking collectives  148 us (45%)
  waiting for transfers between devices  132 us (40%)
  matrix products  24.9 us (8%)
  between operations  13.4 us (4%)
  local copies, waits for them, and re-layouts  8.73 us (3%)
  other arithmetic  3.91 us (1%)
    all_to_all x1, blocking collectives, shards(): lax.all_to_all(jnp.stack([panel] * lax.axis_size('wide')), 'wide', 0, 0)  148 us
    all_gather x1, waiting for transfers between devices, shards(): block_rows = lax.all_gather(standard, 'narrow', axis=0, tiled=True)  132 us
    dot_general x1, matrix products, shards(): lax.dot_general(gathered, block_rows, (((0,), (0,)), ((), ())), preferred...  24.9 us
  transfers between devices with their start and end apart: 1, of which 1 were waited for; matrix products, arithmetic and copies ran while one was open for 0% of the time, Pallas kernels for 0%

profile of v1, /device:TPU:1, one launch (start us, length us, event | category | flops | bytes accessed | tf_op | source)
XLA Modules:
  0.0 331.4 jit_solution(14727873375693200377)
XLA Ops:
  6.5 0.0 all-gather.2.cloned.1.call-start
  6.5 0.7 broadcast_multiply_fusion
  7.2 3.2 select_convert_fusion
  10.5 0.0 all-gather.2.cloned.1.call-update
  10.5 132.5 %all-gather.2.cloned.1.call-done = bf16[2048,1536]{1,0:T(8,128)(2,1)} async-done(((bf16[256,1536]{1,0:T(8,128)(2,1)}), bf16[2048,1536]{1,0:T(8,128)(2,1)}) %all-gather.2.cloned.1.call-update) | async-done | bytes 6291472 | tf_op jit(solution)/shard_map/all_gather | solution.py:20
  143.0 1.8 constant_dynamic-slice_fusion
  144.8 0.5 copy.5
  145.3 6.4 %stack.2 = bf16[16,2048,192]{1,2,0:T(8,128)(2,1)} broadcast(bf16[2048,192]{0,1:T(8,128)(2,1)S(1)} %copy.5), dimensions={1,2} | broadcast | bytes 13369344 | tf_op jit(solution)/shard_map/stack | solution.py:25
  151.7 148.0 %all_to_all.5 = bf16[16,2048,192]{1,2,0:T(8,128)(2,1)S(1)} all-to-all(bf16[16,2048,192]{1,2,0:T(8,128)(2,1)} %stack.2), channel_id=1, replica_groups=mesh['wide'=16,'narrow'=8] {'wide'}, dimensions={0} | all-to-all | bytes 25165824 | tf_op jit(solution)/shard_map/all_to_all | solution.py:25
  299.7 24.9 %convolution_multiply_fusion = f32[3072,1536]{1,0:T(8,128)} fusion(bf16[2048,3072]{0,1:T(8,128)(2,1)S(1)} %bitcast.8, bf16[2048,1536]{1,0:T(8,128)(2,1)} %all-gather.2.cloned.1.call-done), kind=kOutput, calls=%fused_computation | convolution fusion | flops 19332071424 | bytes 37748736 | tf_op jit(solution)/shard_map/dot_general | solution.py:28
  (1 shorter events, 0.0 us)
Async XLA Ops:
  6.5 136.4 %all-gather.2.cloned.1.call-start = ((), (), s32[]{:S(2)}) async-start(), calls=%async_computation.1 | async-start | bytes 7077888 | tf_op jit(solution)/shard_map/all_gather | solution.py:20
Sparse Core Ops, SparseCore 0:
  10.6 132.3 all-gather.1
